TPU v7x, 512 devices: a whole 4x4x16 slice. The times are simulated.
512 devices in a mesh: dp: 32 (over z, core), cent: 16 (over x, y).
Axes of the slice: x: 4, y: 4, z: 16, core: 2. Of those that a mesh axis runs over, the one named last changes fastest.
Arguments:
- embeddings: bfloat16 [262144, 1024], P(('dp', 'cent')), may hold values from -44.5 to 53.875
- centroids: float32 [131072, 1024], P(('dp', 'cent')), may hold values from -3 to 5
- candidates: int32 [1024, 8], P(('dp', 'cent')), may hold values from 0 to 15, all different within a row; in each aligned block of 32 rows (0 to 31, 32 to 63, ...) at most 24 rows name the same one
Outputs:
- new_centroids: float32 [131072, 1024], P(('dp', 'cent'))
- log_norm: float32 [262144], P(('dp', 'cent'))
- objective: float32 [], replicated
Inputs may be any that keep to these rules, and one draw needn't show every extreme that they name: `candidates`: the 8 entries of a row block are different. Among the row blocks of one coarse group (aligned runs of 32 row blocks), no centroid block is named more than 24 times, and some centroid block is named exactly 24 times in every draw.
All inputs are finite; a program needn't handle non-finite values.
Results may differ from a plain program's by a relative error of at most 0.0067.
Values may be sent and summed in bfloat16 or wider, within the bound.
No kernel may reach another device: no remote copies, remote signals or barrier semaphores. Data moves between devices by JAX's collectives and lax.ppermute only.
A program may use at most 128 MiB of HBM per device.

v0:
```python
import math
import jax
import jax.numpy as jnp
from jax import lax
from jax.sharding import PartitionSpec as P

BLK = 256
TOPC = 8
floor_value = -1e30


def per_device(embeddings, centroids, candidates):
    cent_count = lax.axis_size("cent")
    own_index = lax.axis_index("cent")
    block_len = BLK
    feature_dim = embeddings.shape[1]
    own_row_blocks = candidates.shape[0]
    own_blocks = centroids.shape[0] // block_len
    group_blocks = own_row_blocks * cent_count
    slot_count = min(own_row_blocks * cent_count, 3 * own_row_blocks * TOPC // (2 * own_blocks))
    cent_blocks = centroids.astype(jnp.bfloat16).reshape(own_blocks, block_len, feature_dim)
    half_norm = 0.5 * jnp.sum(centroids * centroids, axis=1).reshape(own_blocks, block_len)
    group_rows, group_lists = (
        lax.all_gather(embeddings, "cent", axis=0, tiled=True),
        lax.all_gather(candidates, "cent", axis=0, tiled=True),
    )
    grouped = group_rows.reshape(group_blocks, block_len, feature_dim)
    own_ids = own_index * own_blocks + jnp.arange(own_blocks, dtype=jnp.int32)
    requested = jnp.any(group_lists[:, :, None] == own_ids[None, None, :], axis=1)
    block_iota = jnp.arange(group_blocks, dtype=jnp.int32)
    sort_keys = jnp.where(requested, 0, group_blocks) + block_iota[:, None]
    slot_blocks = jnp.argsort(sort_keys, axis=0)[:slot_count]
    slot_live = jnp.take_along_axis(requested, slot_blocks, axis=0)
    picked = grouped[slot_blocks]
    dot_scores = jnp.einsum(
        "mjbd,jkd->mjbk", picked, cent_blocks, preferred_element_type=jnp.float32
    )
    live_mask = slot_live[:, :, None, None]
    logits = (dot_scores - half_norm[None, :, None, :]) / math.sqrt(feature_dim)
    logits = jnp.where(live_mask, logits, floor_value)
    local_peak = jnp.max(logits, axis=3)
    local_total = jnp.where(
        slot_live[:, :, None], jnp.sum(jnp.exp(logits - local_peak[..., None]), axis=3), 0.0
    )
    peak_rows = (
        jnp.full((group_blocks, block_len), floor_value, jnp.float32)
        .at[slot_blocks]
        .max(local_peak)
    )
    scaled_total = local_total * jnp.exp(local_peak - peak_rows[slot_blocks])
    total_rows = jnp.zeros((group_blocks, block_len), jnp.float32).at[slot_blocks].add(scaled_total)
    global_peak = lax.pmax(peak_rows.astype(jnp.bfloat16), "cent").astype(peak_rows.dtype)
    global_total = lax.psum(total_rows * jnp.exp(peak_rows - global_peak), "cent")
    log_group = global_peak + jnp.log(global_total)
    log_norm = lax.dynamic_slice_in_dim(
        log_group, own_index * own_row_blocks, own_row_blocks, 0
    ).reshape(-1)
    weights = jnp.where(live_mask, jnp.exp(logits - log_group[slot_blocks][..., None]), 0.0)
    counts = jnp.sum(weights, axis=(0, 2))
    weights_bf = weights.astype(jnp.bfloat16)
    block_sums = jnp.einsum(
        "mjbk,mjbd->jkd", weights_bf, picked, preferred_element_type=jnp.float32
    )
    old_blocks = centroids.reshape(own_blocks, block_len, feature_dim)
    new_blocks = (block_sums + old_blocks) / (counts[..., None] + 1.0)
    new_centroids = new_blocks.reshape(own_blocks * block_len, feature_dim)
    row_total_count = embeddings.shape[0] * lax.axis_size("dp") * cent_count
    objective = lax.psum(jnp.sum(log_norm), ("dp", "cent")) / row_total_count
    return (new_centroids, log_norm, objective)


def solution(mesh):
    in_specs = (P(("dp", "cent"), None), P(("dp", "cent"), None), P(("dp", "cent"), None))
    out_specs = (P(("dp", "cent"), None), P(("dp", "cent")), P())
    return jax.shard_map(
        per_device, mesh=mesh, in_specs=in_specs, out_specs=out_specs, check_vma=False
    )
```

profile of v0, /device:TPU:1, one launch (start us, length us, event | category | flops | bytes accessed | tf_op | source)
XLA Modules:
  0.0 435.2 jit_solution(5110639029860988073)
XLA Ops:
  7.2 0.0 all-gather.3.cloned.1.call-start
  7.2 0.7 all-gather.3.cloned.1.call-update
  7.9 19.6 %all-gather = s32[16,2,8]{2,1,0:T(2,128)S(1)} all-gather(s32[1,2,8]{2,1,0:T(2,128)} %bitcast.88), channel_id=1, replica_groups=mesh['dp'=32,'cent'=16] {'cent'}, dimensions={0}, use_global_device_ids=true | all-gather | bytes 1088 | tf_op jit(solution)/shard_map/all_gather | solution.py:25
  27.5 0.4 compare_reduce_fusion
  27.8 0.1 reshape.211
  28.0 0.1 copy.10
  28.1 0.8 sort.17
  28.9 0.1 fusion.37
  29.0 0.7 gather_fusion
  29.7 0.1 copy.11
  29.8 0.1 select_reduce_fusion
  29.9 1.4 multiply_reduce_fusion
  31.3 111.3 %all-gather.3.cloned.1.call-done = bf16[8192,1024]{1,0:T(8,128)(2,1)} async-done(((bf16[512,1024]{1,0:T(8,128)(2,1)}), bf16[8192,1024]{1,0:T(8,128)(2,1)}) %all-gather.3.cloned.1.call-update) | async-done | bytes 16777232 | tf_op jit(solution)/shard_map/all_gather | solution.py:24
  142.6 0.0 copy-start.2
  142.7 12.0 %gather_fusion.1 = bf16[24,256,1024]{2,1,0:T(8,128)(2,1)} fusion(bf16[32,256,1024]{2,1,0:T(8,128)(2,1)} %bitcast.85, s32[1024]{0:T(1024)S(1)} %pad_clamp_fusion), kind=kCustom, calls=%fused_computation.1 | custom fusion | bytes 25165920 | tf_op jit(solution)/shard_map/gather | solution.py:34
  154.6 0.0 copy-done.2
  154.6 6.6 %fusion.11 = (f32[24,256]{1,0:T(8,128)S(1)}, f32[24,256,256]{1,2,0:T(8,128)S(1)}) fusion(f32[256]{0:T(256)S(1)} %broadcast_multiply_fusion, pred[24]{0:T(512)(128)(4,1)S(1)} %select_reduce_fusion, bf16[24,256,1024]{2,1,0:T(8,128)(2,1)} %gather_fusion.1, f32[256,1024]{1,0:T(8,128)S(1)} %copy-done.2), kind=kOutput, calls=%fused_computation.18 | convolution fusion | flops 3227772928 | bytes 19948568 | tf_op jit(solution)/shard_map/mjbd,jkd->mjbk/dot_general | solution.py:35
  161.3 0.0 copy-start
  161.3 2.7 copy-done
  163.9 1.8 exponential_reduce_fusion
  165.8 0.7 scatter_custom_fusion
  166.5 58.2 %pmax.7 = bf16[32,256]{1,0:T(8,128)(2,1)S(1)} all-reduce(bf16[32,256]{1,0:T(8,128)(2,1)S(1)} %convert_element_type.13), channel_id=1, replica_groups=mesh['dp'=32,'cent'=16] {'cent'}, use_global_device_ids=true, to_apply=%region_5.6 | all-reduce | flops 8192 | bytes 32768 | tf_op jit(solution)/shard_map/pmax | solution.py:52
  224.7 0.8 scatter_custom_fusion.1
  225.6 55.6 %psum.14 = f32[32,256]{1,0:T(8,128)S(1)} all-reduce(f32[32,256]{1,0:T(8,128)S(1)} %fusion.27), channel_id=1, replica_groups=mesh['dp'=32,'cent'=16] {'cent'}, use_global_device_ids=true, to_apply=%region_8.9 | all-reduce | flops 8192 | bytes 65536 | tf_op jit(solution)/shard_map/psum | solution.py:53
  281.2 0.6 gather_fusion.2
  281.8 0.0 copy-start.1
  281.8 4.5 %fusion.3 = f32[256]{0:T(256)S(1)} fusion(f32[24,256]{1,0:T(8,128)S(1)} %gather_fusion.2, f32[256]{0:T(256)S(1)} %broadcast_multiply_fusion, f32[24,256,256]{1,2,0:T(8,128)} %copy-done, pred[24]{0:T(512)(128)(4,1)S(1)} %select_reduce_fusion), kind=kLoop, calls=%fused_computation.12 | loop fusion | flops 9436928 | bytes 6318104 | tf_op jit(solution)/shard_map/reduce_sum | solution.py:59
  286.3 0.1 copy-done.1
  286.4 9.3 %fusion.20 = f32[256,1024]{1,0:T(8,128)} fusion(f32[256,1024]{1,0:T(8,128)S(1)} %copy-done.2, bf16[24,256,1024]{2,1,0:T(8,128)(2,1)} %gather_fusion.1, f32[24,256]{1,0:T(8,128)S(1)} %gather_fusion.2, f32[256]{0:T(256)S(1)} %broadcast_multiply_fusion, f32[24,256,256]{1,2,0:T(8,128)S(1)} %copy-done.1, pred[24]{0:T(512)(128)(4,1)S(1)} %select_reduce_fusion, ...), kind=kOutput, calls=%fused_computation.23 | convolution fusion | flops 3231186944 | bytes 20998168 | tf_op jit(solution)/shard_map/mjbk,mjbd->jkd/dot_general | solution.py:61
  295.8 0.6 dynamic-slice_reduce_fusion
  296.4 0.6 copy.12
  296.9 129.6 %psum.15 = f32[]{:T(128)} all-reduce(f32[]{:T(128)} %get-tuple-element.5), channel_id=1, replica_groups=mesh['dp'=32,'cent'=16] {'dp','cent'}, use_global_device_ids=true, to_apply=%region_11.12 | all-reduce | flops 1 | bytes 8 | tf_op jit(solution)/shard_map/psum | solution.py:68
  (9 shorter events, 0.1 us)
Async XLA Ops:
  7.2 135.5 %all-gather.3.cloned.1.call-start = ((), (), s32[]{:S(2)}) async-start(), calls=%async_computation | async-start | bytes 17825792 | tf_op jit(solution)/shard_map/all_gather | solution.py:24
  142.6 12.0 %copy-start.2 = (f32[256,1024]{1,0:T(8,128)S(1)}, f32[256,1024]{1,0:T(8,128)}, u32[]{:S(2)}) copy-start(f32[256,1024]{1,0:T(8,128)} %param.4) | copy-start | bytes 3145732
  161.3 2.7 copy-start
  281.8 4.6 %copy-start.1 = (f32[24,256,256]{1,2,0:T(8,128)S(1)}, f32[24,256,256]{1,2,0:T(8,128)}, u32[]{:S(2)}) copy-start(f32[24,256,256]{1,2,0:T(8,128)} %copy-done) | copy-start | bytes 18874372
Sparse Core Ops, SparseCore 0:
  11.0 131.6 all-gather.2
where the time goes:
time: 436 us; the launch traced here: 435 us
  blocking collectives  263 us (60%)
  waiting for transfers between devices  112 us (26%)
  local copies, waits for them, and re-layouts  16.9 us (4%)
  matrix products  15.9 us (4%)
  between operations  15.9 us (4%)
  other arithmetic  11.3 us (3%)
    psum x1, blocking collectives, per_device(): objective = lax.psum(jnp.sum(log_norm), ('dp', 'cent')) / row_total_count  130 us
    all_gather x1, waiting for transfers between devices, per_device(): lax.all_gather(embeddings, 'cent', axis=0, tiled=True)  111 us
    pmax x1, blocking collectives, per_device(): lax.pmax(peak_rows.astype(jnp.bfloat16), 'cent').astype(peak_rows.dtype)  58.2 us
    psum x1, blocking collectives, per_device(): lax.psum(total_rows * jnp.exp(peak_rows - global_peak), 'cent')  55.6 us
    all_gather x1, blocking collectives, per_device(): lax.all_gather(candidates, 'cent', axis=0, tiled=True)  19.6 us
    gather x1, local copies, waits for them, and re-layouts, per_device(): picked = grouped[slot_blocks]  12 us
    dot_general x1, matrix products, per_device(): jnp.einsum('mjbk,mjbd->jkd', weights_bf, picked, preferred_element_type=j...  9.32 us
  transfers between devices with their start and end apart: 1, of which 1 were waited for; matrix products, arithmetic and copies ran while one was open for 1% of the time, Pallas kernels for 0%

commit v1 on v0

--- a/solution.py
+++ b/solution.py
@@ -22,7 +22,9 @@
     half_norm = 0.5 * jnp.sum(centroids * centroids, axis=1).reshape(own_blocks, block_len)
     group_rows, group_lists = (
         lax.all_gather(embeddings, "cent", axis=0, tiled=True),
-        lax.all_gather(candidates, "cent", axis=0, tiled=True),
+        jnp.concatenate(
+            lax.all_to_all(jnp.stack([candidates] * lax.axis_size("cent")), "cent", 0, 0), axis=0
+        ),
     )
     grouped = group_rows.reshape(group_blocks, block_len, feature_dim)
     own_ids = own_index * own_blocks + jnp.arange(own_blocks, dtype=jnp.int32)

time: 436 us -> 436 us (level)
  blocking collectives: 263 us -> 243 us
  waiting for transfers between devices: 112 us -> 123 us
  starting transfers between devices: 0.04 us -> 7.61 us
    all_gather x1 -> x0, blocking collectives: 19.6 us -> none  [per_device(): lax.all_gather(candidates, 'cent', axis=0, tiled=True)]
    all_to_all x0 -> x1, starting transfers between devices: none -> 7.57 us  [per_device(): lax.all_to_all(jnp.stack([candidates] * lax.axis_size('cent')), 'cent', 0...]
    all_gather x1, waiting for transfers between devices: 111 us -> 117 us  [per_device(): lax.all_gather(embeddings, 'cent', axis=0, tiled=True)]
    all_to_all x0 -> x1, waiting for transfers between devices: none -> 5.07 us  [per_device(): lax.all_to_all(jnp.stack([candidates] * lax.axis_size('cent')), 'cent', 0...]
  transfers between devices with their start and end apart: 1 -> 2, of which waited for: 1 -> 2; matrix products, arithmetic and copies ran while one was open for 1% -> 1% of each run, Pallas kernels for 0% -> 0%
where the time goes in v1:
time: 436 us; the launch traced here: 435 us
  blocking collectives  243 us (56%)
  waiting for transfers between devices  123 us (28%)
  local copies, waits for them, and re-layouts  18.4 us (4%)
  matrix products  15.9 us (4%)
  between operations  15.9 us (4%)
  other arithmetic  11 us (3%)
  starting transfers between devices  7.61 us (2%)
    psum x1, blocking collectives, per_device(): objective = lax.psum(jnp.sum(log_norm), ('dp', 'cent')) / row_total_count  130 us
    all_gather x1, waiting for transfers between devices, per_device(): lax.all_gather(embeddings, 'cent', axis=0, tiled=True)  117 us
    pmax x1, blocking collectives, per_device(): lax.pmax(peak_rows.astype(jnp.bfloat16), 'cent').astype(peak_rows.dtype)  58.2 us
    psum x1, blocking collectives, per_device(): lax.psum(total_rows * jnp.exp(peak_rows - global_peak), 'cent')  55.6 us
    gather x1, local copies, waits for them, and re-layouts, per_device(): picked = grouped[slot_blocks]  12 us
    dot_general x1, matrix products, per_device(): jnp.einsum('mjbk,mjbd->jkd', weights_bf, picked, preferred_element_type=j...  9.3 us
  transfers between devices with their start and end apart: 2, of which 2 were waited for; matrix products, arithmetic and copies ran while one was open for 1% of the time, Pallas kernels for 0%

profile of v1, /device:TPU:1, one launch (start us, length us, event | category | flops | bytes accessed | tf_op | source)
XLA Modules:
  0.0 435.2 jit_solution(3675581800869291137)
XLA Ops:
  7.2 0.0 all-gather.2.cloned.1.call-start
  7.2 0.7 all-gather.2.cloned.1.call-update
  7.9 1.3 stack.2
  9.2 7.6 %all-to-all-start = ((s32[16,2,8]{2,1,0:T(2,128)}), s32[16,2,8]{2,1,0:T(2,128)S(1)}, u32[]{:S(2)}, u32[]{:S(2)}) async-start(s32[16,2,8]{2,1,0:T(2,128)} %stack.2), calls=%async_computation | async-start | bytes 32768 | tf_op jit(solution)/shard_map/all_to_all | solution.py:26
  16.8 1.4 multiply_reduce_fusion
  18.2 5.1 %all-to-all-done = s32[16,2,8]{2,1,0:T(2,128)S(1)} async-done(((s32[16,2,8]{2,1,0:T(2,128)}), s32[16,2,8]{2,1,0:T(2,128)S(1)}, u32[]{:S(2)}, u32[]{:S(2)}) %all-to-all-start) | async-done | bytes 1056 | tf_op jit(solution)/shard_map/all_to_all | solution.py:26
  23.2 0.1 copy.19
  23.3 0.1 copy.22
  23.4 0.1 copy.20
  23.5 0.1 reshape.216
  23.6 0.1 reshape.150
  23.7 0.8 sort.17
  24.5 0.1 fusion.37
  24.6 0.7 gather_fusion
  25.3 0.1 copy.23
  25.4 0.1 select_reduce_fusion
  25.6 117.1 %all-gather.2.cloned.1.call-done = bf16[8192,1024]{1,0:T(8,128)(2,1)} async-done(((bf16[512,1024]{1,0:T(8,128)(2,1)}), bf16[8192,1024]{1,0:T(8,128)(2,1)}) %all-gather.2.cloned.1.call-update) | async-done | bytes 16777232 | tf_op jit(solution)/shard_map/all_gather | solution.py:24
  142.7 0.0 copy-start.2
  142.7 12.0 %gather_fusion.1 = bf16[24,256,1024]{2,1,0:T(8,128)(2,1)} fusion(bf16[32,256,1024]{2,1,0:T(8,128)(2,1)} %bitcast.82, s32[1024]{0:T(1024)S(1)} %pad_clamp_fusion), kind=kCustom, calls=%fused_computation.1 | custom fusion | bytes 25165920 | tf_op jit(solution)/shard_map/gather | solution.py:36
  154.6 0.0 copy-done.2
  154.6 6.6 %fusion.11 = (f32[24,256]{1,0:T(8,128)S(1)}, f32[24,256,256]{1,2,0:T(8,128)S(1)}) fusion(f32[256]{0:T(256)S(1)} %broadcast_multiply_fusion, pred[24]{0:T(512)(128)(4,1)S(1)} %select_reduce_fusion, bf16[24,256,1024]{2,1,0:T(8,128)(2,1)} %gather_fusion.1, f32[256,1024]{1,0:T(8,128)S(1)} %copy-done.2), kind=kOutput, calls=%fused_computation.18 | convolution fusion | flops 3227772928 | bytes 19948568 | tf_op jit(solution)/shard_map/mjbd,jkd->mjbk/dot_general | solution.py:37
  161.3 0.0 copy-start
  161.3 2.7 copy-done
  163.9 1.8 exponential_reduce_fusion
  165.8 0.7 scatter_custom_fusion
  166.5 58.2 %pmax.7 = bf16[32,256]{1,0:T(8,128)(2,1)S(1)} all-reduce(bf16[32,256]{1,0:T(8,128)(2,1)S(1)} %convert_element_type.13), channel_id=1, replica_groups=mesh['dp'=32,'cent'=16] {'cent'}, use_global_device_ids=true, to_apply=%region_5.6 | all-reduce | flops 8192 | bytes 32768 | tf_op jit(solution)/shard_map/pmax | solution.py:54
  224.8 0.8 scatter_custom_fusion.1
  225.6 55.6 %psum.14 = f32[32,256]{1,0:T(8,128)S(1)} all-reduce(f32[32,256]{1,0:T(8,128)S(1)} %fusion.27), channel_id=1, replica_groups=mesh['dp'=32,'cent'=16] {'cent'}, use_global_device_ids=true, to_apply=%region_8.9 | all-reduce | flops 8192 | bytes 65536 | tf_op jit(solution)/shard_map/psum | solution.py:55
  281.2 0.6 gather_fusion.2
  281.8 0.0 copy-start.1
  281.8 4.5 %fusion.3 = f32[256]{0:T(256)S(1)} fusion(f32[24,256]{1,0:T(8,128)S(1)} %gather_fusion.2, f32[256]{0:T(256)S(1)} %broadcast_multiply_fusion, f32[24,256,256]{1,2,0:T(8,128)} %copy-done, pred[24]{0:T(512)(128)(4,1)S(1)} %select_reduce_fusion), kind=kLoop, calls=%fused_computation.12 | loop fusion | flops 9436928 | bytes 6318104 | tf_op jit(solution)/shard_map/reduce_sum | solution.py:61
  286.4 0.1 copy-done.1
  286.5 9.3 %fusion.20 = f32[256,1024]{1,0:T(8,128)} fusion(f32[256,1024]{1,0:T(8,128)S(1)} %copy-done.2, bf16[24,256,1024]{2,1,0:T(8,128)(2,1)} %gather_fusion.1, f32[24,256]{1,0:T(8,128)S(1)} %gather_fusion.2, f32[256]{0:T(256)S(1)} %broadcast_multiply_fusion, f32[24,256,256]{1,2,0:T(8,128)S(1)} %copy-done.1, pred[24]{0:T(512)(128)(4,1)S(1)} %select_reduce_fusion, ...), kind=kOutput, calls=%fused_computation.23 | convolution fusion | flops 3231186944 | bytes 20998168 | tf_op jit(solution)/shard_map/mjbk,mjbd->jkd/dot_general | solution.py:63
  295.8 0.6 dynamic-slice_reduce_fusion
  296.4 0.6 copy.24
  296.9 129.6 %psum.15 = f32[]{:T(128)} all-reduce(f32[]{:T(128)} %get-tuple-element.5), channel_id=1, replica_groups=mesh['dp'=32,'cent'=16] {'dp','cent'}, use_global_device_ids=true, to_apply=%region_11.12 | all-reduce | flops 1 | bytes 8 | tf_op jit(solution)/shard_map/psum | solution.py:70
  (10 shorter events, 0.1 us)
Async XLA Ops:
  7.2 135.5 %all-gather.2.cloned.1.call-start = ((), (), s32[]{:S(2)}) async-start(), calls=%async_computation.1 | async-start | bytes 17825792 | tf_op jit(solution)/shard_map/all_gather | solution.py:24
  9.2 14.0 %all-to-all-start = ((s32[16,2,8]{2,1,0:T(2,128)}), s32[16,2,8]{2,1,0:T(2,128)S(1)}, u32[]{:S(2)}, u32[]{:S(2)}) async-start(s32[16,2,8]{2,1,0:T(2,128)} %stack.2), calls=%async_computation | async-start | bytes 32768 | tf_op jit(solution)/shard_map/all_to_all | solution.py:26
  142.7 12.0 %copy-start.2 = (f32[256,1024]{1,0:T(8,128)S(1)}, f32[256,1024]{1,0:T(8,128)}, u32[]{:S(2)}) copy-start(f32[256,1024]{1,0:T(8,128)} %param.4) | copy-start | bytes 3145732
  161.3 2.7 copy-start
  281.8 4.6 %copy-start.1 = (f32[24,256,256]{1,2,0:T(8,128)S(1)}, f32[24,256,256]{1,2,0:T(8,128)}, u32[]{:S(2)}) copy-start(f32[24,256,256]{1,2,0:T(8,128)} %copy-done) | copy-start | bytes 18874372
Sparse Core Ops, SparseCore 0:
  11.0 131.6 all-gather.1

commit v2 on v0

--- a/solution.py
+++ b/solution.py
@@ -50,7 +50,9 @@
     scaled_total = local_total * jnp.exp(local_peak - peak_rows[slot_blocks])
     total_rows = jnp.zeros((group_blocks, block_len), jnp.float32).at[slot_blocks].add(scaled_total)
     global_peak = lax.pmax(peak_rows.astype(jnp.bfloat16), "cent").astype(peak_rows.dtype)
-    global_total = lax.psum(total_rows * jnp.exp(peak_rows - global_peak), "cent")
+    global_total = jnp.sum(
+        lax.all_gather(total_rows * jnp.exp(peak_rows - global_peak), "cent"), axis=0
+    )
     log_group = global_peak + jnp.log(global_total)
     log_norm = lax.dynamic_slice_in_dim(
         log_group, own_index * own_row_blocks, own_row_blocks, 0

time: 436 us -> 390 us (0.89)
  blocking collectives: 263 us -> 217 us
    psum x1 -> x0, blocking collectives: 55.6 us -> none  [per_device(): lax.psum(total_rows * jnp.exp(peak_rows - global_peak), 'cent')]
    all_gather x0 -> x1, blocking collectives: none -> 16 us  [per_device(): lax.all_gather(total_rows * jnp.exp(peak_rows - global_peak), 'cent')]
    psum x1, blocking collectives: 130 us -> 124 us  [per_device(): objective = lax.psum(jnp.sum(log_norm), ('dp', 'cent')) / row_total_count]
where the time goes in v2:
time: 390 us
  blocking collectives  217 us (56%)
  waiting for transfers between devices  112 us (29%)
  local copies, waits for them, and re-layouts  16.9 us (4%)
  matrix products  15.9 us (4%)
  between operations  15.9 us (4%)
  other arithmetic  11.4 us (3%)
    psum x1, blocking collectives, per_device(): objective = lax.psum(jnp.sum(log_norm), ('dp', 'cent')) / row_total_count  124 us
    all_gather x1, waiting for transfers between devices, per_device(): lax.all_gather(embeddings, 'cent', axis=0, tiled=True)  111 us
    pmax x1, blocking collectives, per_device(): lax.pmax(peak_rows.astype(jnp.bfloat16), 'cent').astype(peak_rows.dtype)  58.2 us
    all_gather x1, blocking collectives, per_device(): lax.all_gather(candidates, 'cent', axis=0, tiled=True)  19.6 us
    all_gather x1, blocking collectives, per_device(): lax.all_gather(total_rows * jnp.exp(peak_rows - global_peak), 'cent')  16 us
    gather x1, local copies, waits for them, and re-layouts, per_device(): picked = grouped[slot_blocks]  12 us
    dot_general x1, matrix products, per_device(): jnp.einsum('mjbk,mjbd->jkd', weights_bf, picked, preferred_element_type=j...  9.32 us
  transfers between devices with their start and end apart: 1, of which 1 were waited for; matrix products, arithmetic and copies ran while one was open for 1% of the time, Pallas kernels for 0%

profile of v2, /device:TPU:1, one launch (start us, length us, event | category | flops | bytes accessed | tf_op | source)
XLA Modules:
  0.0 389.5 jit_solution(532749366786340140)
XLA Ops:
  7.2 0.0 all-gather.4.cloned.1.call-start
  7.2 0.7 all-gather.4.cloned.1.call-update
  7.9 19.6 %all-gather.1 = s32[16,2,8]{2,1,0:T(2,128)S(1)} all-gather(s32[1,2,8]{2,1,0:T(2,128)} %bitcast.90), channel_id=1, replica_groups=mesh['dp'=32,'cent'=16] {'cent'}, dimensions={0}, use_global_device_ids=true | all-gather | bytes 1088 | tf_op jit(solution)/shard_map/all_gather | solution.py:25
  27.5 0.4 compare_reduce_fusion
  27.8 0.1 reshape.212
  28.0 0.1 copy.10
  28.1 0.8 sort.17
  28.9 0.1 fusion.37
  29.0 0.7 gather_fusion
  29.7 0.1 copy.11
  29.8 0.1 select_reduce_fusion
  29.9 1.4 multiply_reduce_fusion
  31.3 111.3 %all-gather.4.cloned.1.call-done = bf16[8192,1024]{1,0:T(8,128)(2,1)} async-done(((bf16[512,1024]{1,0:T(8,128)(2,1)}), bf16[8192,1024]{1,0:T(8,128)(2,1)}) %all-gather.4.cloned.1.call-update) | async-done | bytes 16777232 | tf_op jit(solution)/shard_map/all_gather | solution.py:24
  142.6 0.0 copy-start.2
  142.7 12.0 %gather_fusion.1 = bf16[24,256,1024]{2,1,0:T(8,128)(2,1)} fusion(bf16[32,256,1024]{2,1,0:T(8,128)(2,1)} %bitcast.86, s32[1024]{0:T(1024)S(1)} %pad_clamp_fusion), kind=kCustom, calls=%fused_computation.1 | custom fusion | bytes 25165920 | tf_op jit(solution)/shard_map/gather | solution.py:34
  154.6 0.0 copy-done.2
  154.6 6.6 %fusion.11 = (f32[24,256]{1,0:T(8,128)S(1)}, f32[24,256,256]{1,2,0:T(8,128)S(1)}) fusion(f32[256]{0:T(256)S(1)} %broadcast_multiply_fusion, pred[24]{0:T(512)(128)(4,1)S(1)} %select_reduce_fusion, bf16[24,256,1024]{2,1,0:T(8,128)(2,1)} %gather_fusion.1, f32[256,1024]{1,0:T(8,128)S(1)} %copy-done.2), kind=kOutput, calls=%fused_computation.18 | convolution fusion | flops 3227772928 | bytes 19948568 | tf_op jit(solution)/shard_map/mjbd,jkd->mjbk/dot_general | solution.py:35
  161.3 0.0 copy-start
  161.3 2.7 copy-done
  163.9 1.8 exponential_reduce_fusion
  165.8 0.7 scatter_custom_fusion
  166.5 58.2 %pmax.7 = bf16[32,256]{1,0:T(8,128)(2,1)S(1)} all-reduce(bf16[32,256]{1,0:T(8,128)(2,1)S(1)} %convert_element_type.13), channel_id=1, replica_groups=mesh['dp'=32,'cent'=16] {'cent'}, use_global_device_ids=true, to_apply=%region_5.6 | all-reduce | flops 8192 | bytes 32768 | tf_op jit(solution)/shard_map/pmax | solution.py:52
  224.7 0.8 scatter_custom_fusion.1
  225.6 16.0 %all-gather = f32[512,256]{1,0:T(8,128)S(1)} all-gather(f32[32,256]{1,0:T(8,128)S(1)} %fusion.27), channel_id=2, replica_groups=mesh['dp'=32,'cent'=16] {'cent'}, dimensions={0}, use_global_device_ids=true | all-gather | bytes 557056 | tf_op jit(solution)/shard_map/all_gather | solution.py:54
  241.6 0.6 gather_fusion.2
  242.2 0.0 copy-start.1
  242.2 4.5 %fusion.3 = f32[256]{0:T(256)S(1)} fusion(f32[24,256]{1,0:T(8,128)S(1)} %gather_fusion.2, f32[256]{0:T(256)S(1)} %broadcast_multiply_fusion, f32[24,256,256]{1,2,0:T(8,128)} %copy-done, pred[24]{0:T(512)(128)(4,1)S(1)} %select_reduce_fusion), kind=kLoop, calls=%fused_computation.12 | loop fusion | flops 9436928 | bytes 6318104 | tf_op jit(solution)/shard_map/reduce_sum | solution.py:61
  246.8 0.1 copy-done.1
  246.9 9.3 %fusion.20 = f32[256,1024]{1,0:T(8,128)} fusion(f32[256,1024]{1,0:T(8,128)S(1)} %copy-done.2, bf16[24,256,1024]{2,1,0:T(8,128)(2,1)} %gather_fusion.1, f32[24,256]{1,0:T(8,128)S(1)} %gather_fusion.2, f32[256]{0:T(256)S(1)} %broadcast_multiply_fusion, f32[24,256,256]{1,2,0:T(8,128)S(1)} %copy-done.1, pred[24]{0:T(512)(128)(4,1)S(1)} %select_reduce_fusion, ...), kind=kOutput, calls=%fused_computation.23 | convolution fusion | flops 3231186944 | bytes 20998168 | tf_op jit(solution)/shard_map/mjbk,mjbd->jkd/dot_general | solution.py:63
  256.2 0.6 dynamic-slice_reduce_fusion
  256.8 0.6 copy.12
  257.4 123.5 %psum.7 = f32[]{:T(128)} all-reduce(f32[]{:T(128)} %get-tuple-element.5), channel_id=1, replica_groups=mesh['dp'=32,'cent'=16] {'dp','cent'}, use_global_device_ids=true, to_apply=%region_11.12 | all-reduce | flops 1 | bytes 8 | tf_op jit(solution)/shard_map/psum | solution.py:70
  (10 shorter events, 0.1 us)
Async XLA Ops:
  7.2 135.5 %all-gather.4.cloned.1.call-start = ((), (), s32[]{:S(2)}) async-start(), calls=%async_computation | async-start | bytes 17825792 | tf_op jit(solution)/shard_map/all_gather | solution.py:24
  142.6 12.0 %copy-start.2 = (f32[256,1024]{1,0:T(8,128)S(1)}, f32[256,1024]{1,0:T(8,128)}, u32[]{:S(2)}) copy-start(f32[256,1024]{1,0:T(8,128)} %param.4) | copy-start | bytes 3145732
  161.3 2.7 copy-start
  242.2 4.6 %copy-start.1 = (f32[24,256,256]{1,2,0:T(8,128)S(1)}, f32[24,256,256]{1,2,0:T(8,128)}, u32[]{:S(2)}) copy-start(f32[24,256,256]{1,2,0:T(8,128)} %copy-done) | copy-start | bytes 18874372
Sparse Core Ops, SparseCore 0:
  11.0 131.6 all-gather.3
